TPU v7x, 128 devices: a whole 4x4x4 slice. The times are simulated.
128 devices in a mesh: grp: 64 (over z, y, x), sub: 2 (over core).
Axes of the slice: x: 4, y: 4, z: 4, core: 2. Of those that a mesh axis runs over, the one named last changes fastest.
Arguments:
- potentials: bfloat16 [4096, 200, 200], P(('grp', 'sub')), may hold values from -6 to 6
- dimers: int32 [16384, 2], P(('grp', 'sub')), may hold values from 0 to 4095, as said below
- coupling: float32 [16384], P(('grp', 'sub')), may hold values from 0.3 to 1.5
- transform: bfloat16 [400, 400], replicated, may hold values from -0.3125 to 0.3125
Outputs:
- energies: float32 [16384, 400], P(('grp', 'sub'))
- checksum: float32 [1], replicated
Inputs may be any that keep to these rules, and one draw needn't show every extreme that they name: `dimers`: each row names two different fragments. Rows d with d // 128 = o belong to owner o, and their second fragment f has f // 32 = o. Among the 128 first fragments of one owner's rows, at most 2 fall into the fragments of any one device (fragments f with f // 32 equal), and exactly 2 into some device's fragments.
All inputs are finite; a program needn't handle non-finite values.
Results may differ from a plain program's by a relative error of at most 0.0023.
Values may be sent and summed in bfloat16 or wider, within the bound.
A program may use at most 192 MiB of HBM per device.

v0:
```python
import jax
import jax.numpy as jnp
from jax import lax
from jax.sharding import Mesh
from jax.sharding import PartitionSpec as P

GRP_SUB = ("grp_0", "grp_1", "grp_2", "sub")


def in_blocks(value, dim, peers):
    before, after = (value.shape[:dim], value.shape[dim + 1 :])
    return jnp.moveaxis(value.reshape(*before, peers, -1, *after), dim, 0)


def edges_of(length, count):
    unit = 8 if length >= 8 * count else 1
    return [length // unit * k // count * unit for k in range(1, count)]


def in_order(tiles, dim):
    tiles = jnp.moveaxis(tiles, 0, dim)
    shape = tiles.shape
    return tiles.reshape(*shape[:dim], shape[dim] * shape[dim + 1], *shape[dim + 2 :])


def several_exchanges(value, axis, pieces, split_dim, concat_dim):
    tiles = in_blocks(value, split_dim, lax.axis_size(axis))
    widest = max(range(1, max(2, tiles.ndim - 1)), key=lambda d: tiles.shape[d])
    done = []
    for section in jnp.split(tiles, edges_of(tiles.shape[widest], pieces), axis=widest):
        if section.size:
            done.append(lax.all_to_all(section, axis, split_axis=0, concat_axis=0, tiled=True))
    return in_order(jnp.concatenate(done, axis=widest), concat_dim)


def over_axes(value, axes):
    for axis in axes:
        value = lax.psum(value, axis)
    return value


def block_energies(left, right, scale, transform, basis):
    upper = transform[:basis]
    lower = transform[basis:]
    cross = jnp.einsum("nab,nbc->nac", left, right, preferred_element_type=jnp.float32)
    block = (cross * (scale[:, None, None] / jnp.sqrt(jnp.float32(basis)))).astype(jnp.bfloat16)
    top = jnp.einsum("nab,bk->nak", left, upper, preferred_element_type=jnp.float32)
    top = top + jnp.einsum("nab,bk->nak", block, lower, preferred_element_type=jnp.float32)
    bottom = jnp.einsum("nab,ak->nbk", block, upper, preferred_element_type=jnp.float32)
    bottom = bottom + jnp.einsum("nab,bk->nak", right, lower, preferred_element_type=jnp.float32)
    upper_f = upper.astype(jnp.float32)
    lower_f = lower.astype(jnp.float32)
    return jnp.sum(upper_f[None] * top, axis=1) + jnp.sum(lower_f[None] * bottom, axis=1)


def local(potentials, dimers, coupling, transform):
    frag_dev, basis, _ = potentials.shape
    count = dimers.shape[0]
    owners = lax.axis_size(GRP_SUB)
    cap = max(2, (4 * count + 3 * owners - 1) // (3 * owners))
    wanted = dimers[:, 0]
    source = wanted // frag_dev
    onehot = (source[:, None] == jnp.arange(owners, dtype=jnp.int32)[None, :]).astype(jnp.int32)
    ranking = jnp.sum(jnp.cumsum(onehot, axis=0) * onehot, axis=1) - 1
    slots = source * cap + ranking
    requests = jnp.zeros((owners * cap,), jnp.int32).at[slots].set(wanted % frag_dev)
    asked = lax.all_to_all(
        requests.reshape(owners, cap), GRP_SUB, split_axis=0, concat_axis=0, tiled=True
    )
    served = jnp.take(potentials, asked.reshape(-1), axis=0).reshape(owners, cap, basis, basis)
    arrived = several_exchanges(served, GRP_SUB, 2, 0, 0)
    leading = jnp.take(arrived.reshape(owners * cap, basis, basis), slots, axis=0)
    trailing = jnp.take(potentials, dimers[:, 1] % frag_dev, axis=0)
    width = 8
    leading = leading.reshape(count // width, width, basis, basis)
    trailing = trailing.reshape(count // width, width, basis, basis)
    scales = coupling.reshape(count // width, width)

    def one_block(item):
        left, right, scale = item
        return block_energies(left, right, scale, transform, basis)

    energies = lax.map(one_block, (leading, trailing, scales)).reshape(count, 2 * basis)
    total = count * owners
    position = lax.axis_index(GRP_SUB) * count + jnp.arange(count, dtype=jnp.int32)
    weights = (position.astype(jnp.float32) + 1.0) / total
    partial_value = 2.0 / total * jnp.sum(weights * jnp.mean(energies * energies, axis=1))
    checksum = over_axes(partial_value, GRP_SUB)
    return (energies, checksum.reshape(1))


def solution(mesh):
    split = Mesh(
        mesh.devices.reshape(4, 4, 4, mesh.shape["sub"]), ("grp_0", "grp_1", "grp_2", "sub")
    )
    return jax.shard_map(
        local,
        mesh=split,
        in_specs=(P(GRP_SUB, None, None), P(GRP_SUB, None), P(GRP_SUB), P()),
        out_specs=(P(GRP_SUB, None), P()),
        check_vma=False,
    )
```

profile of v0, /device:TPU:1, one launch (start us, length us, event | category | flops | bytes accessed | tf_op | source)
XLA Modules:
  0.0 635.7 jit_solution(10583920919584439760)
XLA Ops:
  5.2 20.9 %all_to_all.19 = s32[128,1,2]{2,1,0:T(1,128)S(1)} all-to-all(s32[128,1,2]{2,1,0:T(1,128)S(1)} %bitcast.76), channel_id=1, replica_groups=mesh['grp_0'=4,'grp_1'=4,'grp_2'=4,'sub'=2] {'grp_0','grp_1','grp_2','sub'}, dimensions={0} | all-to-all | bytes 2048 | tf_op jit(solution)/shard_map/all_to_all | solution.py:67
  27.8 12.6 %gather_fusion = bf16[256,200,200]{2,1,0:T(8,128)(2,1)} fusion(bf16[32,200,200]{2,1,0:T(8,128)(2,1)S(1)} %copy-done, s32[1024]{0:T(1024)S(1)} %pad_clamp_fusion.2), kind=kCustom, calls=%fused_computation | custom fusion | bytes 40961024 | tf_op jit(solution)/shard_map/jit(_take)/gather | solution.py:70
  40.4 18.3 %broadcast_select_fusion = bf16[128,1,2,200,200]{4,3,2,1,0:T(8,128)(2,1)} fusion(bf16[128,1,2,200,200]{4,3,2,1,0:T(8,128)(2,1)} %bitcast.70, pred[128,2]{1,0:T(8,128)(4,1)S(1)} %compare_and_fusion), kind=kLoop, calls=%fused_computation.35 | loop fusion | flops 10240000 | bytes 40960256 | tf_op jit(solution)/shard_map/jit(_take)/select_n | solution.py:70
  58.7 11.0 %split.8 = bf16[128,1,2,96,200]{4,3,2,1,0:T(8,128)(2,1)} slice(bf16[128,1,2,200,200]{4,3,2,1,0:T(8,128)(2,1)} %broadcast_select_fusion), slice={[0:128], [0:1], [0:2], [0:96], [0:200]} | slice | bytes 19660800 | tf_op jit(solution)/shard_map/split | solution.py:30
  69.6 5.5 all-to-all-start.1
  75.1 12.2 %split.9 = bf16[128,1,2,104,200]{4,3,2,1,0:T(8,128)(2,1)} slice(bf16[128,1,2,200,200]{4,3,2,1,0:T(8,128)(2,1)} %broadcast_select_fusion), slice={[0:128], [0:1], [0:2], [96:200], [0:200]} | slice | bytes 21299200 | tf_op jit(solution)/shard_map/split | solution.py:30
  87.3 18.8 %copy.31 = bf16[128,1,2,104,200]{3,4,2,1,0:T(8,128)(2,1)} copy(bf16[128,1,2,104,200]{4,3,2,1,0:T(8,128)(2,1)} %split.9) | data formatting | bytes 21299200 | tf_op jit(solution)/shard_map/split | solution.py:30
  106.1 121.2 %all-to-all-done.1 = bf16[128,1,2,96,200]{4,3,2,1,0:T(8,128)(2,1)} async-done(((bf16[128,1,2,96,200]{4,3,2,1,0:T(8,128)(2,1)}), bf16[128,1,2,96,200]{4,3,2,1,0:T(8,128)(2,1)}, u32[]{:S(2)}, u32[]{:S(2)}) %all-to-all-start.1) | async-done | bytes 9830432 | tf_op jit(solution)/shard_map/all_to_all | solution.py:32
  227.3 24.5 %all-to-all-start.2 = ((bf16[128,1,2,104,200]{3,4,2,1,0:T(8,128)(2,1)}), bf16[128,1,2,104,200]{3,4,2,1,0:T(8,128)(2,1)}, u32[]{:S(2)}, u32[]{:S(2)}) async-start(bf16[128,1,2,104,200]{3,4,2,1,0:T(8,128)(2,1)} %copy.31), calls=%async_computation.2 | async-start | bytes 26214400 | tf_op jit(solution)/shard_map/all_to_all | solution.py:32
  252.6 8.7 %gather_fusion.2 = bf16[128,200,200]{2,1,0:T(8,128)(2,1)} fusion(bf16[32,200,200]{2,1,0:T(8,128)(2,1)S(1)} %copy-done, s32[1024]{0:T(1024)S(1)} %pad_clamp_fusion), kind=kCustom, calls=%fused_computation.2 | custom fusion | bytes 20480512 | tf_op jit(solution)/shard_map/jit(_take)/gather | solution.py:73
  262.1 10.1 %broadcast_select_fusion.1 = bf16[16,8,200,200]{3,2,1,0:T(8,128)(2,1)} fusion(bf16[16,8,200,200]{3,2,1,0:T(8,128)(2,1)} %bitcast.73, pred[16,8]{1,0:T(8,128)(4,1)S(1)} %broadcast_in_dim.59), kind=kLoop, calls=%fused_computation.36 | loop fusion | flops 5120000 | bytes 20480128 | tf_op jit(solution)/shard_map/jit(_take)/select_n | solution.py:73
  272.3 17.3 %copy.32 = bf16[128,1,2,96,200]{3,4,2,1,0:T(8,128)(2,1)} copy(bf16[128,1,2,96,200]{4,3,2,1,0:T(8,128)(2,1)} %all-to-all-done.1) | data formatting | bytes 19660800 | tf_op jit(solution)/shard_map/all_to_all | solution.py:32
  289.6 123.4 %all-to-all-done.2 = bf16[128,1,2,104,200]{3,4,2,1,0:T(8,128)(2,1)} async-done(((bf16[128,1,2,104,200]{3,4,2,1,0:T(8,128)(2,1)}), bf16[128,1,2,104,200]{3,4,2,1,0:T(8,128)(2,1)}, u32[]{:S(2)}, u32[]{:S(2)}) %all-to-all-start.2) | async-done | bytes 10649632 | tf_op jit(solution)/shard_map/all_to_all | solution.py:32
  413.1 18.7 %pad_maximum_fusion = bf16[128,1,2,200,200]{3,4,2,1,0:T(8,128)(2,1)} fusion(bf16[128,1,2,104,200]{3,4,2,1,0:T(8,128)(2,1)} %all-to-all-done.2, bf16[128,1,2,96,200]{3,4,2,1,0:T(8,128)(2,1)} %copy.32), kind=kLoop, calls=%fused_computation.34 | loop fusion | flops 40960000 | bytes 40960000 | tf_op jit(solution)/shard_map/concatenate | solution.py:33
  431.7 17.1 %gather_fusion.1 = bf16[128,200,200]{1,2,0:T(8,128)(2,1)} fusion(bf16[256,200,200]{1,2,0:T(8,128)(2,1)} %bitcast.71, s32[1024]{0:T(1024)S(1)} %pad_clamp_fusion.1), kind=kCustom, calls=%fused_computation.1 | custom fusion | bytes 20480512 | tf_op jit(solution)/shard_map/jit(_take)/gather | solution.py:72
  448.9 17.9 %copy.33 = bf16[128,200,200]{2,1,0:T(8,128)(2,1)} copy(bf16[128,200,200]{1,2,0:T(8,128)(2,1)} %gather_fusion.1) | data formatting | bytes 20480000 | tf_op jit(solution)/shard_map/jit(_take)/gather | solution.py:72
  466.8 10.3 %broadcast_select_fusion.2 = bf16[16,8,200,200]{3,2,1,0:T(8,128)(2,1)} fusion(bf16[16,8,200,200]{3,2,1,0:T(8,128)(2,1)} %bitcast.72, pred[16,8]{1,0:T(8,128)(4,1)S(1)} %broadcast_in_dim.51), kind=kLoop, calls=%fused_computation.37 | loop fusion | flops 5120000 | bytes 20480128 | tf_op jit(solution)/shard_map/jit(_take)/select_n | solution.py:72
  477.0 110.3 %while.10 = (s32[]{:T(128)}, f32[16,8,400]{2,1,0:T(8,128)S(1)}, bf16[400,400]{1,0:T(8,128)(2,1)S(1)}, bf16[16,8,200,200]{3,2,1,0:T(8,128)(2,1)}, bf16[16,8,200,2...) while((s32[]{:T(128)}, f32[16,8,400]{2,1,0:T(8,128)S(1)}, bf16[400,400]{1,0:T(8,128)(2,1)S(1)}, ...), condition=%wide.region_6.7_spmd, body=%wide.region_3.6_spmd.sunk | while | flops 1156636800 | bytes 19904180 | solution.py:83
  477.0 1.8 multiply_convert_fusion.2
  482.0 1.9 multiply_reduce_fusion.7
  483.9 1.8 multiply_convert_fusion.2
  485.7 1.7 fusion.54
  488.9 1.9 multiply_reduce_fusion.7
  490.8 1.8 multiply_convert_fusion.2
  492.6 1.7 fusion.54
  495.8 1.9 multiply_reduce_fusion.7
  497.7 1.8 multiply_convert_fusion.2
  499.5 1.7 fusion.54
  502.7 1.9 multiply_reduce_fusion.7
  504.6 1.8 multiply_convert_fusion.2
  506.4 1.7 fusion.54
  509.6 1.9 multiply_reduce_fusion.7
  511.5 1.8 multiply_convert_fusion.2
  513.3 1.7 fusion.54
  516.5 1.9 multiply_reduce_fusion.7
  518.4 1.8 multiply_convert_fusion.2
  520.2 1.7 fusion.54
  523.4 1.9 multiply_reduce_fusion.7
  525.3 1.8 multiply_convert_fusion.2
  530.3 1.9 multiply_reduce_fusion.7
  532.2 1.8 multiply_convert_fusion.2
  537.2 1.9 multiply_reduce_fusion.7
  539.1 1.8 multiply_convert_fusion.2
  544.1 1.9 multiply_reduce_fusion.7
  546.0 1.8 multiply_convert_fusion.2
  551.0 1.9 multiply_reduce_fusion.7
  552.9 1.8 multiply_convert_fusion.2
  554.7 1.7 fusion.54
  557.9 1.9 multiply_reduce_fusion.7
  559.8 1.8 multiply_convert_fusion.2
  561.6 1.7 fusion.54
  564.8 1.9 multiply_reduce_fusion.7
  566.7 1.8 multiply_convert_fusion.2
  568.5 1.7 fusion.54
  571.7 1.9 multiply_reduce_fusion.7
  573.6 1.8 multiply_convert_fusion.2
  575.4 1.7 fusion.54
  578.6 1.9 multiply_reduce_fusion.7
  580.5 1.8 multiply_convert_fusion.2
  585.5 1.9 multiply_reduce_fusion.7
  589.0 11.9 %psum.28 = f32[]{:T(128)} all-reduce(f32[]{:T(128)S(6)} %mul_shard_map.3), channel_id=1, replica_groups=mesh['grp_0'=4,'grp_1'=4,'grp_2'=4,'sub'=2] {'grp_0'}, use_global_device_ids=true, to_apply=%region_9.10 | all-reduce | flops 1 | bytes 8 | tf_op jit(solution)/shard_map/psum | solution.py:38
  600.9 13.8 %psum.29 = f32[]{:T(128)} all-reduce(f32[]{:T(128)} %psum.28), channel_id=1, replica_groups=mesh['grp_0'=4,'grp_1'=4,'grp_2'=4,'sub'=2] {'grp_1'}, use_global_device_ids=true, to_apply=%region_10.11 | all-reduce | flops 1 | bytes 8 | tf_op jit(solution)/shard_map/psum | solution.py:38
  614.7 11.1 %psum.30 = f32[]{:T(128)} all-reduce(f32[]{:T(128)} %psum.29), channel_id=1, replica_groups=mesh['grp_0'=4,'grp_1'=4,'grp_2'=4,'sub'=2] {'grp_2'}, use_global_device_ids=true, to_apply=%region_11.12 | all-reduce | flops 1 | bytes 8 | tf_op jit(solution)/shard_map/psum | solution.py:38
  625.7 9.2 %psum.31 = f32[1]{0:T(128)} all-reduce(f32[1]{0:T(128)} %bitcast.19), channel_id=1, replica_groups=mesh['grp_0'=4,'grp_1'=4,'grp_2'=4,'sub'=2] {'sub'}, use_global_device_ids=true, to_apply=%region_12.13 | all-reduce | flops 1 | bytes 8 | tf_op jit(solution)/shard_map/psum | solution.py:38
  (116 shorter events, 43.3 us)
Async XLA Ops:
  0.6 27.1 %copy-start = (bf16[32,200,200]{2,1,0:T(8,128)(2,1)S(1)}, bf16[32,200,200]{2,1,0:T(8,128)(2,1)}, u32[]{:S(2)}) copy-start(bf16[32,200,200]{2,1,0:T(8,128)(2,1)} %param.6) | copy-start | bytes 7680004
  69.6 157.7 %all-to-all-start.1 = ((bf16[128,1,2,96,200]{4,3,2,1,0:T(8,128)(2,1)}), bf16[128,1,2,96,200]{4,3,2,1,0:T(8,128)(2,1)}, u32[]{:S(2)}, u32[]{:S(2)}) async-start(bf16[128,1,2,96,200]{4,3,2,1,0:T(8,128)(2,1)} %split.8), calls=%async_computation.1 | async-start | bytes 25165824 | tf_op jit(solution)/shard_map/all_to_all | solution.py:32
  227.3 185.7 %all-to-all-start.2 = ((bf16[128,1,2,104,200]{3,4,2,1,0:T(8,128)(2,1)}), bf16[128,1,2,104,200]{3,4,2,1,0:T(8,128)(2,1)}, u32[]{:S(2)}, u32[]{:S(2)}) async-start(bf16[128,1,2,104,200]{3,4,2,1,0:T(8,128)(2,1)} %copy.31), calls=%async_computation.2 | async-start | bytes 26214400 | tf_op jit(solution)/shard_map/all_to_all | solution.py:32
  466.7 10.3 %copy-start.2 = (bf16[400,400]{1,0:T(8,128)(2,1)S(1)}, bf16[400,400]{1,0:T(8,128)(2,1)}, u32[]{:S(2)}) copy-start(bf16[400,400]{1,0:T(8,128)(2,1)} %param.9) | copy-start | bytes 960004
  587.4 48.4 %copy-start.1 = (bf16[32,200,200]{2,1,0:T(8,128)(2,1)S(1)}, bf16[32,200,200]{2,1,0:T(8,128)(2,1)}, u32[]{:S(2)}) copy-start(bf16[32,200,200]{2,1,0:T(8,128)(2,1)} %param.6) | copy-start | bytes 7680004
where the time goes:
time: 639 us; the launch traced here: 636 us
  waiting for transfers between devices  245 us (38%)
  local copies, waits for them, and re-layouts  119 us (19%)
  matrix products  108 us (17%)
  blocking collectives  66.8 us (10%)
  other arithmetic  64.7 us (10%)
  starting transfers between devices  30 us (5%)
    all_to_all x2, waiting for transfers between devices, several_exchanges(): lax.all_to_all(section, axis, split_axis=0, concat_axis=0, tiled=True)  245 us
    psum x4, blocking collectives, over_axes(): value = lax.psum(value, axis)  45.9 us
    split x3, local copies, waits for them, and re-layouts, several_exchanges(): jnp.split(tiles, edges_of(tiles.shape[widest], pieces), axis=widest)  41.9 us
    gather x2, local copies, waits for them, and re-layouts, local(): jnp.take(arrived.reshape(owners * cap, basis, basis), slots, axis=0)  35 us
    all_to_all x2, starting transfers between devices, several_exchanges(): lax.all_to_all(section, axis, split_axis=0, concat_axis=0, tiled=True)  30 us
    dot_general x16, matrix products, block_energies(): jnp.einsum('nab,bk->nak', right, lower, preferred_element_type=jnp.float32)  29.7 us
    dot_general x16, matrix products, block_energies(): jnp.einsum('nab,nbc->nac', left, right, preferred_element_type=jnp.float32)  28.3 us
    dot_general x16, matrix products, block_energies(): jnp.einsum('nab,bk->nak', left, upper, preferred_element_type=jnp.float32)  27.7 us
  transfers between devices with their start and end apart: 2, of which 2 were waited for; matrix products, arithmetic and copies ran while one was open for 11% of the time, Pallas kernels for 0%

commit v1 on v0

--- a/solution.py
+++ b/solution.py
@@ -35,7 +35,7 @@
 
 def over_axes(value, axes):
     for axis in axes:
-        value = lax.psum(value, axis)
+        value = jnp.sum(lax.all_gather(value, axis_name=axis), 0)
     return value
 
 

time: 639 us -> 647 us (1.013)
  local copies, waits for them, and re-layouts: 119 us -> 128 us
    psum x4 -> x0, blocking collectives: 45.9 us -> none  [over_axes(): value = lax.psum(value, axis)]
    unnamed x0 -> x4, blocking collectives: none -> 43.5 us
    unnamed x7 -> x21, local copies, waits for them, and re-layouts: 0.83 us -> 10.1 us
where the time goes in v1:
time: 647 us; the launch traced here: 643 us
  waiting for transfers between devices  243 us (38%)
  local copies, waits for them, and re-layouts  128 us (20%)
  matrix products  108 us (17%)
  other arithmetic  67.1 us (10%)
  blocking collectives  64.4 us (10%)
  starting transfers between devices  30 us (5%)
    all_to_all x2, waiting for transfers between devices, several_exchanges(): lax.all_to_all(section, axis, split_axis=0, concat_axis=0, tiled=True)  243 us
    unnamed x4, blocking collectives  43.5 us
    split x3, local copies, waits for them, and re-layouts, several_exchanges(): jnp.split(tiles, edges_of(tiles.shape[widest], pieces), axis=widest)  41.9 us
    gather x2, local copies, waits for them, and re-layouts, local(): jnp.take(arrived.reshape(owners * cap, basis, basis), slots, axis=0)  34.8 us
    all_to_all x2, starting transfers between devices, several_exchanges(): lax.all_to_all(section, axis, split_axis=0, concat_axis=0, tiled=True)  30 us
    dot_general x16, matrix products, block_energies(): jnp.einsum('nab,bk->nak', right, lower, preferred_element_type=jnp.float32)  29.7 us
    dot_general x16, matrix products, block_energies(): jnp.einsum('nab,nbc->nac', left, right, preferred_element_type=jnp.float32)  28.3 us
    dot_general x16, matrix products, block_energies(): jnp.einsum('nab,bk->nak', left, upper, preferred_element_type=jnp.float32)  27.7 us
  transfers between devices with their start and end apart: 2, of which 2 were waited for; matrix products, arithmetic and copies ran while one was open for 11% of the time, Pallas kernels for 0%

profile of v1, /device:TPU:1, one launch (start us, length us, event | category | flops | bytes accessed | tf_op | source)
XLA Modules:
  0.0 643.5 jit_solution(12241140137679793305)
XLA Ops:
  5.2 20.9 %all_to_all.19 = s32[128,1,2]{2,1,0:T(1,128)S(1)} all-to-all(s32[128,1,2]{2,1,0:T(1,128)S(1)} %bitcast.84), channel_id=1, replica_groups=mesh['grp_0'=4,'grp_1'=4,'grp_2'=4,'sub'=2] {'grp_0','grp_1','grp_2','sub'}, dimensions={0} | all-to-all | bytes 2048 | tf_op jit(solution)/shard_map/all_to_all | solution.py:67
  27.8 12.6 %gather_fusion = bf16[256,200,200]{2,1,0:T(8,128)(2,1)} fusion(bf16[32,200,200]{2,1,0:T(8,128)(2,1)S(1)} %copy-done, s32[1024]{0:T(1024)S(1)} %pad_clamp_fusion.2), kind=kCustom, calls=%fused_computation | custom fusion | bytes 40961024 | tf_op jit(solution)/shard_map/jit(_take)/gather | solution.py:70
  40.4 18.3 %broadcast_select_fusion = bf16[128,1,2,200,200]{4,3,2,1,0:T(8,128)(2,1)} fusion(bf16[128,1,2,200,200]{4,3,2,1,0:T(8,128)(2,1)} %bitcast.78, pred[128,2]{1,0:T(8,128)(4,1)S(1)} %compare_and_fusion), kind=kLoop, calls=%fused_computation.35 | loop fusion | flops 10240000 | bytes 40960256 | tf_op jit(solution)/shard_map/jit(_take)/select_n | solution.py:70
  58.7 11.0 %split.8 = bf16[128,1,2,96,200]{4,3,2,1,0:T(8,128)(2,1)} slice(bf16[128,1,2,200,200]{4,3,2,1,0:T(8,128)(2,1)} %broadcast_select_fusion), slice={[0:128], [0:1], [0:2], [0:96], [0:200]} | slice | bytes 19660800 | tf_op jit(solution)/shard_map/split | solution.py:30
  69.6 5.5 all-to-all-start.1
  75.1 12.2 %split.9 = bf16[128,1,2,104,200]{4,3,2,1,0:T(8,128)(2,1)} slice(bf16[128,1,2,200,200]{4,3,2,1,0:T(8,128)(2,1)} %broadcast_select_fusion), slice={[0:128], [0:1], [0:2], [96:200], [0:200]} | slice | bytes 21299200 | tf_op jit(solution)/shard_map/split | solution.py:30
  87.3 18.8 %copy.31 = bf16[128,1,2,104,200]{3,4,2,1,0:T(8,128)(2,1)} copy(bf16[128,1,2,104,200]{4,3,2,1,0:T(8,128)(2,1)} %split.9) | data formatting | bytes 21299200 | tf_op jit(solution)/shard_map/split | solution.py:30
  106.1 121.2 %all-to-all-done.1 = bf16[128,1,2,96,200]{4,3,2,1,0:T(8,128)(2,1)} async-done(((bf16[128,1,2,96,200]{4,3,2,1,0:T(8,128)(2,1)}), bf16[128,1,2,96,200]{4,3,2,1,0:T(8,128)(2,1)}, u32[]{:S(2)}, u32[]{:S(2)}) %all-to-all-start.1) | async-done | bytes 9830432 | tf_op jit(solution)/shard_map/all_to_all | solution.py:32
  227.3 24.5 %all-to-all-start.2 = ((bf16[128,1,2,104,200]{3,4,2,1,0:T(8,128)(2,1)}), bf16[128,1,2,104,200]{3,4,2,1,0:T(8,128)(2,1)}, u32[]{:S(2)}, u32[]{:S(2)}) async-start(bf16[128,1,2,104,200]{3,4,2,1,0:T(8,128)(2,1)} %copy.31), calls=%async_computation.2 | async-start | bytes 26214400 | tf_op jit(solution)/shard_map/all_to_all | solution.py:32
  252.6 8.7 %gather_fusion.2 = bf16[128,200,200]{2,1,0:T(8,128)(2,1)} fusion(bf16[32,200,200]{2,1,0:T(8,128)(2,1)S(1)} %copy-done, s32[1024]{0:T(1024)S(1)} %pad_clamp_fusion), kind=kCustom, calls=%fused_computation.2 | custom fusion | bytes 20480512 | tf_op jit(solution)/shard_map/jit(_take)/gather | solution.py:73
  263.4 10.1 %broadcast_select_fusion.1 = bf16[16,8,200,200]{3,2,1,0:T(8,128)(2,1)} fusion(bf16[16,8,200,200]{3,2,1,0:T(8,128)(2,1)} %bitcast.81, pred[16,8]{1,0:T(8,128)(4,1)S(1)} %broadcast_in_dim.59), kind=kLoop, calls=%fused_computation.36 | loop fusion | flops 5120000 | bytes 20480128 | tf_op jit(solution)/shard_map/jit(_take)/select_n | solution.py:73
  273.5 17.3 %copy.32 = bf16[128,1,2,96,200]{3,4,2,1,0:T(8,128)(2,1)} copy(bf16[128,1,2,96,200]{4,3,2,1,0:T(8,128)(2,1)} %all-to-all-done.1) | data formatting | bytes 19660800 | tf_op jit(solution)/shard_map/all_to_all | solution.py:32
  290.9 122.2 %all-to-all-done.2 = bf16[128,1,2,104,200]{3,4,2,1,0:T(8,128)(2,1)} async-done(((bf16[128,1,2,104,200]{3,4,2,1,0:T(8,128)(2,1)}), bf16[128,1,2,104,200]{3,4,2,1,0:T(8,128)(2,1)}, u32[]{:S(2)}, u32[]{:S(2)}) %all-to-all-start.2) | async-done | bytes 10649632 | tf_op jit(solution)/shard_map/all_to_all | solution.py:32
  413.1 18.7 %pad_maximum_fusion = bf16[128,1,2,200,200]{3,4,2,1,0:T(8,128)(2,1)} fusion(bf16[128,1,2,104,200]{3,4,2,1,0:T(8,128)(2,1)} %all-to-all-done.2, bf16[128,1,2,96,200]{3,4,2,1,0:T(8,128)(2,1)} %copy.32), kind=kLoop, calls=%fused_computation.34 | loop fusion | flops 40960000 | bytes 40960000 | tf_op jit(solution)/shard_map/concatenate | solution.py:33
  431.7 17.1 %gather_fusion.1 = bf16[128,200,200]{1,2,0:T(8,128)(2,1)} fusion(bf16[256,200,200]{1,2,0:T(8,128)(2,1)} %bitcast.79, s32[1024]{0:T(1024)S(1)} %pad_clamp_fusion.1), kind=kCustom, calls=%fused_computation.1 | custom fusion | bytes 20480512 | tf_op jit(solution)/shard_map/jit(_take)/gather | solution.py:72
  448.9 17.7 %copy.33 = bf16[128,200,200]{2,1,0:T(8,128)(2,1)} copy(bf16[128,200,200]{1,2,0:T(8,128)(2,1)} %gather_fusion.1) | data formatting | bytes 20480000 | tf_op jit(solution)/shard_map/jit(_take)/gather | solution.py:72
  466.5 10.2 %broadcast_select_fusion.2 = bf16[16,8,200,200]{3,2,1,0:T(8,128)(2,1)} fusion(bf16[16,8,200,200]{3,2,1,0:T(8,128)(2,1)} %bitcast.80, pred[16,8]{1,0:T(8,128)(4,1)S(1)} %broadcast_in_dim.51), kind=kLoop, calls=%fused_computation.37 | loop fusion | flops 5120000 | bytes 20480128 | tf_op jit(solution)/shard_map/jit(_take)/select_n | solution.py:72
  476.8 110.3 %while.10 = (s32[]{:T(128)}, f32[16,8,400]{2,1,0:T(8,128)S(1)}, bf16[400,400]{1,0:T(8,128)(2,1)S(1)}, bf16[16,8,200,200]{3,2,1,0:T(8,128)(2,1)}, bf16[16,8,200,2...) while((s32[]{:T(128)}, f32[16,8,400]{2,1,0:T(8,128)S(1)}, bf16[400,400]{1,0:T(8,128)(2,1)S(1)}, ...), condition=%wide.region_6.7_spmd, body=%wide.region_3.6_spmd.sunk | while | flops 1156636800 | bytes 19904180 | solution.py:83
  476.8 1.8 multiply_convert_fusion.2
  478.6 1.7 fusion.54
  481.8 1.9 multiply_reduce_fusion.7
  483.7 1.8 multiply_convert_fusion.2
  485.4 1.7 fusion.54
  488.7 1.9 multiply_reduce_fusion.7
  490.6 1.8 multiply_convert_fusion.2
  492.3 1.7 fusion.54
  495.6 1.9 multiply_reduce_fusion.7
  497.5 1.8 multiply_convert_fusion.2
  499.2 1.7 fusion.54
  502.5 1.9 multiply_reduce_fusion.7
  504.4 1.8 multiply_convert_fusion.2
  509.4 1.9 multiply_reduce_fusion.7
  511.3 1.8 multiply_convert_fusion.2
  516.2 1.9 multiply_reduce_fusion.7
  518.2 1.8 multiply_convert_fusion.2
  523.1 1.9 multiply_reduce_fusion.7
  525.1 1.8 multiply_convert_fusion.2
  526.8 1.7 fusion.54
  530.0 1.9 multiply_reduce_fusion.7
  532.0 1.8 multiply_convert_fusion.2
  533.7 1.7 fusion.54
  536.9 1.9 multiply_reduce_fusion.7
  538.8 1.8 multiply_convert_fusion.2
  540.6 1.7 fusion.54
  543.8 1.9 multiply_reduce_fusion.7
  545.7 1.8 multiply_convert_fusion.2
  547.5 1.7 fusion.54
  550.7 1.9 multiply_reduce_fusion.7
  552.6 1.8 multiply_convert_fusion.2
  554.4 1.7 fusion.54
  557.6 1.9 multiply_reduce_fusion.7
  559.5 1.8 multiply_convert_fusion.2
  561.3 1.7 fusion.54
  564.5 1.9 multiply_reduce_fusion.7
  566.4 1.8 multiply_convert_fusion.2
  571.4 1.9 multiply_reduce_fusion.7
  573.3 1.8 multiply_convert_fusion.2
  578.3 1.9 multiply_reduce_fusion.7
  580.2 1.8 multiply_convert_fusion.2
  585.2 1.9 multiply_reduce_fusion.7
  590.8 11.3 %all-reduce = f32[4]{0:T(128)S(1)} all-reduce(f32[4]{0:T(128)S(1)} %dynamic-update-slice), channel_id=1, replica_groups=mesh['grp_0'=4,'grp_1'=4,'grp_2'=4,'sub'=2] {'grp_0'}, use_global_device_ids=true, to_apply=%add | all-reduce | flops 4 | bytes 32
  605.3 13.2 %all-reduce.1 = f32[4]{0:T(128)S(1)} all-reduce(f32[4]{0:T(128)S(1)} %dynamic-update-slice.1), channel_id=1, replica_groups=mesh['grp_0'=4,'grp_1'=4,'grp_2'=4,'sub'=2] {'grp_1'}, use_global_device_ids=true, to_apply=%add.1 | all-reduce | flops 4 | bytes 32
  621.1 10.4 %all-reduce.2 = f32[4]{0:T(128)S(1)} all-reduce(f32[4]{0:T(128)S(1)} %dynamic-update-slice.2), channel_id=1, replica_groups=mesh['grp_0'=4,'grp_1'=4,'grp_2'=4,'sub'=2] {'grp_2'}, use_global_device_ids=true, to_apply=%add.2 | all-reduce | flops 4 | bytes 32
  633.5 8.6 %all-reduce.3 = f32[2]{0:T(128)S(1)} all-reduce(f32[2]{0:T(128)S(1)} %dynamic-update-slice.3), channel_id=1, replica_groups=mesh['grp_0'=4,'grp_1'=4,'grp_2'=4,'sub'=2] {'sub'}, use_global_device_ids=true, to_apply=%add.3 | all-reduce | flops 2 | bytes 16
  (134 shorter events, 55.0 us)
Async XLA Ops:
  0.6 27.1 %copy-start = (bf16[32,200,200]{2,1,0:T(8,128)(2,1)S(1)}, bf16[32,200,200]{2,1,0:T(8,128)(2,1)}, u32[]{:S(2)}) copy-start(bf16[32,200,200]{2,1,0:T(8,128)(2,1)} %param.6) | copy-start | bytes 7680004
  69.6 157.7 %all-to-all-start.1 = ((bf16[128,1,2,96,200]{4,3,2,1,0:T(8,128)(2,1)}), bf16[128,1,2,96,200]{4,3,2,1,0:T(8,128)(2,1)}, u32[]{:S(2)}, u32[]{:S(2)}) async-start(bf16[128,1,2,96,200]{4,3,2,1,0:T(8,128)(2,1)} %split.8), calls=%async_computation.1 | async-start | bytes 25165824 | tf_op jit(solution)/shard_map/all_to_all | solution.py:32
  227.3 185.7 %all-to-all-start.2 = ((bf16[128,1,2,104,200]{3,4,2,1,0:T(8,128)(2,1)}), bf16[128,1,2,104,200]{3,4,2,1,0:T(8,128)(2,1)}, u32[]{:S(2)}, u32[]{:S(2)}) async-start(bf16[128,1,2,104,200]{3,4,2,1,0:T(8,128)(2,1)} %copy.31), calls=%async_computation.2 | async-start | bytes 26214400 | tf_op jit(solution)/shard_map/all_to_all | solution.py:32
  466.5 10.2 %copy-start.2 = (bf16[400,400]{1,0:T(8,128)(2,1)S(1)}, bf16[400,400]{1,0:T(8,128)(2,1)}, u32[]{:S(2)}) copy-start(bf16[400,400]{1,0:T(8,128)(2,1)} %param.9) | copy-start | bytes 960004
  476.8 143.8 %copy-start.3 = (u32[128]{0:T(128)S(1)}, u32[128]{0:T(128)}, u32[]{:S(2)}) copy-start(u32[128]{0:T(128)} %constant.153) | copy-start | bytes 1540
  587.1 56.4 %copy-start.1 = (bf16[32,200,200]{2,1,0:T(8,128)(2,1)S(1)}, bf16[32,200,200]{2,1,0:T(8,128)(2,1)}, u32[]{:S(2)}) copy-start(bf16[32,200,200]{2,1,0:T(8,128)(2,1)} %param.6) | copy-start | bytes 7680004
